TPU v7x, 128 devices: a whole 4x4x4 slice. The times are simulated.
128 devices in a mesh: req: 16 (over z, x), ctx: 8 (over y, core).
Axes of the slice: x: 4, y: 4, z: 4, core: 2. Of those that a mesh axis runs over, the one named last changes fastest.
Arguments:
- item_table: bfloat16 [32768, 256], P('req'), may hold values from -6 to 6
- cand_owner: int32 [16, 512, 1], P('req'), may hold values from 0 to 15; in each aligned block of 64 rows (0 to 63, 64 to 127, ..., all dimensions but the last counted through in order) at most 8 rows name the same one
- cand_slot: int32 [16, 512], P('req'), may hold values from 0 to 2047
- w_in: bfloat16 [256, 1024], replicated, may hold values from -0.375 to 0.375
- w_uq: bfloat16 [1024, 2048], replicated, may hold values from -0.1875 to 0.1875
- w_out: bfloat16 [1024, 1024], replicated, may hold values from -0.1875 to 0.1875
- k_cache: bfloat16 [16, 32768, 1024], P('req', 'ctx'), may hold values from -12 to 12
- v_cache: bfloat16 [16, 32768, 1024], P('req', 'ctx'), may hold values from -6 to 6
- hist_len: int32 [16], P('req'), may hold values from 2048 to 32768, as said below
Outputs:
- ranked: bfloat16 [16, 512, 1024], P('req', 'ctx')
Inputs may be any that keep to these rules, and one draw needn't show every extreme that they name: `cand_owner`: in each aligned block of 512 / 8 candidates of a user, no owner is named more than 8 times, and in some block one owner is named exactly 8 times. `hist_len`: in every draw some user has the full 32768 events.
All inputs are finite; a program needn't handle non-finite values.
Results may differ from a plain program's by a relative error of at most 0.014.
Values may be sent and summed in bfloat16 or wider, within the bound.
A program may use at most 128 MiB of HBM per device.

v0:
```python
import jax
import jax.numpy as jnp
from jax import lax
from jax.sharding import PartitionSpec as P

HEADS = 8


def from_everyone(shard, axis):
    size = lax.axis_size(axis)
    return lax.all_to_all(
        jnp.broadcast_to(shard[None], (size, *shard.shape)), axis, 0, 0, tiled=True
    )


def joined_along(parts, dim):
    parts = jnp.moveaxis(parts, 0, dim)
    dims = parts.shape
    return parts.reshape(*dims[:dim], dims[dim] * dims[dim + 1], *dims[dim + 2 :])


def collect(shard, axis, dim):
    parts = from_everyone(shard, axis)
    return joined_along(parts, dim)


def split_up(shard, dim, size):
    dims = shard.shape
    parts = shard.reshape(*dims[:dim], size, dims[dim] // size, *dims[dim + 1 :])
    return jnp.moveaxis(parts, dim, 0)


def summed_on_arrival(shard, axis, dim):
    size = lax.axis_size(axis)
    parts = lax.all_to_all(split_up(shard, dim, size), axis, 0, 0, tiled=True)
    return jnp.sum(parts, axis=0)


def layer_norm(values):
    centre = jnp.mean(values, axis=-1, keepdims=True)
    centred = values - centre
    spread = jnp.mean(centred * centred, axis=-1, keepdims=True)
    return centred * lax.rsqrt(spread + 1e-05)


def fetch_rows(owners, slot_ids, item_table, capacity):
    owner_count = lax.axis_size("req")
    matches = (owners[:, None] == jnp.arange(owner_count, dtype=jnp.int32)[None, :]).astype(
        jnp.int32
    )
    ranking = jnp.sum((jnp.cumsum(matches, axis=0) - 1) * matches, axis=1)
    outgoing = jnp.zeros((owner_count, capacity), jnp.int32).at[owners, ranking].set(slot_ids)
    looked_up = item_table[lax.all_to_all(outgoing, "req", split_axis=0, concat_axis=0, tiled=True)]
    returned = lax.all_to_all(looked_up, "req", split_axis=0, concat_axis=0, tiled=True)
    return returned[owners, ranking]


def attend_rows(queries, keys_local, values_local, length, offset):
    row_count, width = queries.shape
    head_dim = width // HEADS
    scale = head_dim ** (-0.5)
    block_keys = min(512, keys_local.shape[0])
    total_blocks = keys_local.shape[0] // block_keys
    query_heads = queries.reshape(row_count, HEADS, head_dim)

    def step(index, running):
        start = index * block_keys
        key_block = lax.dynamic_slice_in_dim(keys_local, start, block_keys, 0).reshape(
            block_keys, HEADS, head_dim
        )
        value_block = lax.dynamic_slice_in_dim(values_local, start, block_keys, 0).reshape(
            block_keys, HEADS, head_dim
        )
        scores = (
            jnp.einsum("qhd,khd->hqk", query_heads, key_block, preferred_element_type=jnp.float32)
            * scale
        )
        position = offset + start + jnp.arange(block_keys, dtype=jnp.int32)
        weights = jnp.where(position[None, None, :] < length, jax.nn.silu(scores), 0.0).astype(
            jnp.bfloat16
        )
        added = jnp.einsum("hqk,khd->qhd", weights, value_block, preferred_element_type=jnp.float32)
        return running + added.reshape(row_count, width)

    live_blocks = jnp.clip((length - offset + block_keys - 1) // block_keys, 0, total_blocks)
    return lax.fori_loop(0, live_blocks, step, jnp.zeros((row_count, width), jnp.float32))


def shards(item_table, cand_owner, cand_slot, w_in, w_uq, w_out, k_cache, v_cache, hist_len):
    width = w_out.shape[0]
    ctx_count = lax.axis_size("ctx")
    ctx_index = lax.axis_index("ctx")
    per_device = cand_owner.shape[1] // ctx_count
    capacity_base = max(2, 2 * per_device // lax.axis_size("req"))
    owners_all = cand_owner[0, :, 0]
    slots_all = cand_slot[0]
    my_start = ctx_index * per_device
    my_owners = lax.dynamic_slice_in_dim(owners_all, my_start, per_device, 0)
    my_slots = lax.dynamic_slice_in_dim(slots_all, my_start, per_device, 0)
    embedded = fetch_rows(my_owners, my_slots, item_table, capacity_base)
    features = jnp.dot(embedded, w_in, preferred_element_type=jnp.float32).astype(jnp.bfloat16)
    normed = layer_norm(features.astype(jnp.float32)).astype(jnp.bfloat16)
    projected = jax.nn.silu(jnp.dot(normed, w_uq, preferred_element_type=jnp.float32)).astype(
        jnp.bfloat16
    )
    features, gate_u, query_mine = (features, projected[:, :width], projected[:, width:])
    queries = collect(query_mine, "ctx", 0)
    length = hist_len[0]
    keys_local = k_cache[0]
    values_local = v_cache[0]
    offset = ctx_index * keys_local.shape[0]
    attended = summed_on_arrival(
        attend_rows(queries, keys_local, values_local, length, offset), "ctx", 0
    )
    mixed = (layer_norm(attended) * gate_u.astype(jnp.float32)).astype(jnp.bfloat16)
    ranked = features.astype(jnp.float32) + jnp.dot(
        mixed, w_out, preferred_element_type=jnp.float32
    )
    return ranked.astype(jnp.bfloat16)[None]


def solution(mesh):
    in_specs = (
        P("req", None),
        P("req", None, None),
        P("req", None),
        P(),
        P(),
        P(),
        P("req", "ctx", None),
        P("req", "ctx", None),
        P("req"),
    )
    out_specs = P("req", "ctx", None)
    return jax.shard_map(shards, mesh=mesh, in_specs=in_specs, out_specs=out_specs, check_vma=False)
```

profile of v0, /device:TPU:1, one launch (start us, length us, event | category | flops | bytes accessed | tf_op | source)
XLA Modules:
  0.0 219.4 jit_solution(8853719524996504243)
XLA Ops:
  2.7 3.5 %scatter_fusion = s32[16,8]{0,1:T(8,128)S(1)} fusion(s32[16,8]{0,1:T(8,128)S(1)} %broadcast.122, s32[64]{0:T(128)S(1)} %get-tuple-element.83, s32[64]{0:T(128)S(1)} %dynamic-slice_bitcast_fusion), kind=kCustom, calls=%fused_computation.2 | custom fusion | bytes 1280 | tf_op jit(solution)/shard_map/scatter | solution.py:52
  6.3 14.6 %all_to_all.27 = s32[16,1,8]{2,1,0:T(1,128)S(1)} all-to-all(s32[16,1,8]{2,1,0:T(1,128)S(1)} %copy.22), channel_id=1, replica_groups=mesh['req'=16,'ctx'=8] {'req'}, dimensions={0} | all-to-all | bytes 1024 | tf_op jit(solution)/shard_map/all_to_all | solution.py:53
  23.3 9.2 %all_to_all.28 = bf16[16,8,256]{2,1,0:T(8,128)(2,1)S(1)} all-to-all(bf16[16,8,256]{2,1,0:T(8,128)(2,1)S(1)} %bitcast.90), channel_id=1, replica_groups=mesh['req'=16,'ctx'=8] {'req'}, dimensions={0} | all-to-all | bytes 131072 | tf_op jit(solution)/shard_map/all_to_all | solution.py:54
  34.9 3.1 %multiply_convert_fusion = bf16[64,2048]{1,0:T(8,128)(2,1)S(1)} fusion(bf16[1024,2048]{1,0:T(8,128)(2,1)} %param.15, f32[64,1024]{1,0:T(8,128)S(1)} %get-tuple-element.88, f32[64]{0:T(128)S(1)} %add_rsqrt_fusion.1, f32[64]{0:T(128)S(1)} %broadcast_multiply_fusion.1), kind=kOutput, calls=%fused_computation.24 | convolution fusion | flops 269287424 | bytes 4719104 | tf_op jit(solution)/shard_map/dot_general | solution.py:103
  39.9 8.0 %all-to-all-start.2 = ((bf16[8,64,1024]{2,1,0:T(8,128)(2,1)}), bf16[8,64,1024]{2,1,0:T(8,128)(2,1)S(1)}, u32[]{:S(2)}, u32[]{:S(2)}) async-start(bf16[8,64,1024]{2,1,0:T(8,128)(2,1)} %broadcast_in_dim.15), calls=%async_computation.2 | async-start | bytes 2097152 | tf_op jit(solution)/shard_map/all_to_all | solution.py:11
  48.5 11.5 %copy.26 = bf16[1,4096,1024]{1,2,0:T(8,128)(2,1)} copy(bf16[1,4096,1024]{2,1,0:T(8,128)(2,1)} %param.17) | data formatting | bytes 16777216 | tf_op args[6]
  60.1 11.3 %copy.25 = bf16[1,4096,1024]{1,2,0:T(8,128)(2,1)} copy(bf16[1,4096,1024]{2,1,0:T(8,128)(2,1)} %param.18) | data formatting | bytes 16777216 | tf_op args[7]
  74.3 109.3 %while.10 = (s32[]{:T(128)}, f32[512,1024]{0,1:T(8,128)}, s32[]{:T(128)}, bf16[4096,1024]{0,1:T(8,128)(2,1)}, s32[]{:T(128)}, /*index=5*/s32[]{:T(128)}, bf16[40...) while((s32[]{:T(128)}, f32[512,1024]{0,1:T(8,128)}, ...), condition=%wide.region_6.7_spmd, body=%wide.region_5.6_spmd.sunk | while | flops 1088947200 | bytes 15729851 | solution.py:86
  75.0 2.7 %constant_dynamic-slice_fusion.4 = (bf16[512,1024]{0,1:T(8,128)(2,1)S(1)}, bf16[512,1024]{0,1:T(8,128)(2,1)}) fusion(bf16[4096,1024]{0,1:T(8,128)(2,1)} %get-tuple-element.173, s32[]{:T(128)S(6)} %select_n.74, bf16[4096,1024]{0,1:T(8,128)(2,1)} %get-tuple-element.170), kind=kLoop, calls=%fused_computation.14.clone.1 | loop fusion | bytes 4194308 | tf_op jit(solution)/shard_map/while/body/dynamic_slice | solution.py:68
  77.7 6.3 %fusion.44 = f32[8,128,512]{2,1,0:T(8,128)} fusion(bf16[512,8,128]{0,2,1:T(8,128)(2,1)} %bitcast.83, pred[512]{0:T(512)(128)(4,1)S(1)} %add_compare_fusion.2, bf16[512,8,128]{0,2,1:T(8,128)(2,1)S(1)} %bitcast.82, bf16[512,8,128]{2,0,1:T(8,128)(2,1)} %get-tuple-element.174), kind=kOutput, calls=%fused_computation.10.clone.1 | convolution fusion | flops 1088421888 | bytes 5243392 | tf_op jit(solution)/shard_map/while/body/hqk,khd->qhd/dot_general | solution.py:82
  84.0 4.0 %bitcast_add_fusion.2 = f32[512,1024]{0,1:T(8,128)} fusion(f32[512,1024]{0,1:T(8,128)} %get-tuple-element.156, f32[8,128,512]{2,1,0:T(8,128)} %fusion.44), kind=kLoop, calls=%fused_computation.12.clone.1 | loop fusion | flops 524288 | bytes 6291456 | tf_op jit(solution)/shard_map/while/body/add | solution.py:83
  88.6 2.7 %constant_dynamic-slice_fusion.4 = (bf16[512,1024]{0,1:T(8,128)(2,1)S(1)}, bf16[512,1024]{0,1:T(8,128)(2,1)}) fusion(bf16[4096,1024]{0,1:T(8,128)(2,1)} %get-tuple-element.173, s32[]{:T(128)S(6)} %select_n.74, bf16[4096,1024]{0,1:T(8,128)(2,1)} %get-tuple-element.170), kind=kLoop, calls=%fused_computation.14.clone.1 | loop fusion | bytes 4194308 | tf_op jit(solution)/shard_map/while/body/dynamic_slice | solution.py:68
  91.3 6.3 %fusion.44 = f32[8,128,512]{2,1,0:T(8,128)} fusion(bf16[512,8,128]{0,2,1:T(8,128)(2,1)} %bitcast.83, pred[512]{0:T(512)(128)(4,1)S(1)} %add_compare_fusion.2, bf16[512,8,128]{0,2,1:T(8,128)(2,1)S(1)} %bitcast.82, bf16[512,8,128]{2,0,1:T(8,128)(2,1)} %get-tuple-element.174), kind=kOutput, calls=%fused_computation.10.clone.1 | convolution fusion | flops 1088421888 | bytes 5243392 | tf_op jit(solution)/shard_map/while/body/hqk,khd->qhd/dot_general | solution.py:82
  97.6 4.0 %bitcast_add_fusion.2 = f32[512,1024]{0,1:T(8,128)} fusion(f32[512,1024]{0,1:T(8,128)} %get-tuple-element.156, f32[8,128,512]{2,1,0:T(8,128)} %fusion.44), kind=kLoop, calls=%fused_computation.12.clone.1 | loop fusion | flops 524288 | bytes 6291456 | tf_op jit(solution)/shard_map/while/body/add | solution.py:83
  102.3 2.7 %constant_dynamic-slice_fusion.4 = (bf16[512,1024]{0,1:T(8,128)(2,1)S(1)}, bf16[512,1024]{0,1:T(8,128)(2,1)}) fusion(bf16[4096,1024]{0,1:T(8,128)(2,1)} %get-tuple-element.173, s32[]{:T(128)S(6)} %select_n.74, bf16[4096,1024]{0,1:T(8,128)(2,1)} %get-tuple-element.170), kind=kLoop, calls=%fused_computation.14.clone.1 | loop fusion | bytes 4194308 | tf_op jit(solution)/shard_map/while/body/dynamic_slice | solution.py:68
  105.0 6.3 %fusion.44 = f32[8,128,512]{2,1,0:T(8,128)} fusion(bf16[512,8,128]{0,2,1:T(8,128)(2,1)} %bitcast.83, pred[512]{0:T(512)(128)(4,1)S(1)} %add_compare_fusion.2, bf16[512,8,128]{0,2,1:T(8,128)(2,1)S(1)} %bitcast.82, bf16[512,8,128]{2,0,1:T(8,128)(2,1)} %get-tuple-element.174), kind=kOutput, calls=%fused_computation.10.clone.1 | convolution fusion | flops 1088421888 | bytes 5243392 | tf_op jit(solution)/shard_map/while/body/hqk,khd->qhd/dot_general | solution.py:82
  111.3 4.0 %bitcast_add_fusion.2 = f32[512,1024]{0,1:T(8,128)} fusion(f32[512,1024]{0,1:T(8,128)} %get-tuple-element.156, f32[8,128,512]{2,1,0:T(8,128)} %fusion.44), kind=kLoop, calls=%fused_computation.12.clone.1 | loop fusion | flops 524288 | bytes 6291456 | tf_op jit(solution)/shard_map/while/body/add | solution.py:83
  115.9 2.7 %constant_dynamic-slice_fusion.4 = (bf16[512,1024]{0,1:T(8,128)(2,1)S(1)}, bf16[512,1024]{0,1:T(8,128)(2,1)}) fusion(bf16[4096,1024]{0,1:T(8,128)(2,1)} %get-tuple-element.173, s32[]{:T(128)S(6)} %select_n.74, bf16[4096,1024]{0,1:T(8,128)(2,1)} %get-tuple-element.170), kind=kLoop, calls=%fused_computation.14.clone.1 | loop fusion | bytes 4194308 | tf_op jit(solution)/shard_map/while/body/dynamic_slice | solution.py:68
  118.6 6.3 %fusion.44 = f32[8,128,512]{2,1,0:T(8,128)} fusion(bf16[512,8,128]{0,2,1:T(8,128)(2,1)} %bitcast.83, pred[512]{0:T(512)(128)(4,1)S(1)} %add_compare_fusion.2, bf16[512,8,128]{0,2,1:T(8,128)(2,1)S(1)} %bitcast.82, bf16[512,8,128]{2,0,1:T(8,128)(2,1)} %get-tuple-element.174), kind=kOutput, calls=%fused_computation.10.clone.1 | convolution fusion | flops 1088421888 | bytes 5243392 | tf_op jit(solution)/shard_map/while/body/hqk,khd->qhd/dot_general | solution.py:82
  124.9 4.0 %bitcast_add_fusion.2 = f32[512,1024]{0,1:T(8,128)} fusion(f32[512,1024]{0,1:T(8,128)} %get-tuple-element.156, f32[8,128,512]{2,1,0:T(8,128)} %fusion.44), kind=kLoop, calls=%fused_computation.12.clone.1 | loop fusion | flops 524288 | bytes 6291456 | tf_op jit(solution)/shard_map/while/body/add | solution.py:83
  132.3 6.3 %fusion.44 = f32[8,128,512]{2,1,0:T(8,128)} fusion(bf16[512,8,128]{0,2,1:T(8,128)(2,1)} %bitcast.83, pred[512]{0:T(512)(128)(4,1)S(1)} %add_compare_fusion.2, bf16[512,8,128]{0,2,1:T(8,128)(2,1)S(1)} %bitcast.82, bf16[512,8,128]{2,0,1:T(8,128)(2,1)} %get-tuple-element.174), kind=kOutput, calls=%fused_computation.10.clone.1 | convolution fusion | flops 1088421888 | bytes 5243392 | tf_op jit(solution)/shard_map/while/body/hqk,khd->qhd/dot_general | solution.py:82
  138.6 4.0 %bitcast_add_fusion.2 = f32[512,1024]{0,1:T(8,128)} fusion(f32[512,1024]{0,1:T(8,128)} %get-tuple-element.156, f32[8,128,512]{2,1,0:T(8,128)} %fusion.44), kind=kLoop, calls=%fused_computation.12.clone.1 | loop fusion | flops 524288 | bytes 6291456 | tf_op jit(solution)/shard_map/while/body/add | solution.py:83
  143.3 2.7 %constant_dynamic-slice_fusion.4 = (bf16[512,1024]{0,1:T(8,128)(2,1)S(1)}, bf16[512,1024]{0,1:T(8,128)(2,1)}) fusion(bf16[4096,1024]{0,1:T(8,128)(2,1)} %get-tuple-element.173, s32[]{:T(128)S(6)} %select_n.74, bf16[4096,1024]{0,1:T(8,128)(2,1)} %get-tuple-element.170), kind=kLoop, calls=%fused_computation.14.clone.1 | loop fusion | bytes 4194308 | tf_op jit(solution)/shard_map/while/body/dynamic_slice | solution.py:68
  146.0 6.3 %fusion.44 = f32[8,128,512]{2,1,0:T(8,128)} fusion(bf16[512,8,128]{0,2,1:T(8,128)(2,1)} %bitcast.83, pred[512]{0:T(512)(128)(4,1)S(1)} %add_compare_fusion.2, bf16[512,8,128]{0,2,1:T(8,128)(2,1)S(1)} %bitcast.82, bf16[512,8,128]{2,0,1:T(8,128)(2,1)} %get-tuple-element.174), kind=kOutput, calls=%fused_computation.10.clone.1 | convolution fusion | flops 1088421888 | bytes 5243392 | tf_op jit(solution)/shard_map/while/body/hqk,khd->qhd/dot_general | solution.py:82
  152.3 4.0 %bitcast_add_fusion.2 = f32[512,1024]{0,1:T(8,128)} fusion(f32[512,1024]{0,1:T(8,128)} %get-tuple-element.156, f32[8,128,512]{2,1,0:T(8,128)} %fusion.44), kind=kLoop, calls=%fused_computation.12.clone.1 | loop fusion | flops 524288 | bytes 6291456 | tf_op jit(solution)/shard_map/while/body/add | solution.py:83
  159.6 6.3 %fusion.44 = f32[8,128,512]{2,1,0:T(8,128)} fusion(bf16[512,8,128]{0,2,1:T(8,128)(2,1)} %bitcast.83, pred[512]{0:T(512)(128)(4,1)S(1)} %add_compare_fusion.2, bf16[512,8,128]{0,2,1:T(8,128)(2,1)S(1)} %bitcast.82, bf16[512,8,128]{2,0,1:T(8,128)(2,1)} %get-tuple-element.174), kind=kOutput, calls=%fused_computation.10.clone.1 | convolution fusion | flops 1088421888 | bytes 5243392 | tf_op jit(solution)/shard_map/while/body/hqk,khd->qhd/dot_general | solution.py:82
  165.9 4.0 %bitcast_add_fusion.2 = f32[512,1024]{0,1:T(8,128)} fusion(f32[512,1024]{0,1:T(8,128)} %get-tuple-element.156, f32[8,128,512]{2,1,0:T(8,128)} %fusion.44), kind=kLoop, calls=%fused_computation.12.clone.1 | loop fusion | flops 524288 | bytes 6291456 | tf_op jit(solution)/shard_map/while/body/add | solution.py:83
  170.6 2.7 %constant_dynamic-slice_fusion.4 = (bf16[512,1024]{0,1:T(8,128)(2,1)S(1)}, bf16[512,1024]{0,1:T(8,128)(2,1)}) fusion(bf16[4096,1024]{0,1:T(8,128)(2,1)} %get-tuple-element.173, s32[]{:T(128)S(6)} %select_n.74, bf16[4096,1024]{0,1:T(8,128)(2,1)} %get-tuple-element.170), kind=kLoop, calls=%fused_computation.14.clone.1 | loop fusion | bytes 4194308 | tf_op jit(solution)/shard_map/while/body/dynamic_slice | solution.py:68
  173.3 6.3 %fusion.44 = f32[8,128,512]{2,1,0:T(8,128)} fusion(bf16[512,8,128]{0,2,1:T(8,128)(2,1)} %bitcast.83, pred[512]{0:T(512)(128)(4,1)S(1)} %add_compare_fusion.2, bf16[512,8,128]{0,2,1:T(8,128)(2,1)S(1)} %bitcast.82, bf16[512,8,128]{2,0,1:T(8,128)(2,1)} %get-tuple-element.174), kind=kOutput, calls=%fused_computation.10.clone.1 | convolution fusion | flops 1088421888 | bytes 5243392 | tf_op jit(solution)/shard_map/while/body/hqk,khd->qhd/dot_general | solution.py:82
  179.6 4.0 %bitcast_add_fusion.2 = f32[512,1024]{0,1:T(8,128)} fusion(f32[512,1024]{0,1:T(8,128)} %get-tuple-element.156, f32[8,128,512]{2,1,0:T(8,128)} %fusion.44), kind=kLoop, calls=%fused_computation.12.clone.1 | loop fusion | flops 524288 | bytes 6291456 | tf_op jit(solution)/shard_map/while/body/add | solution.py:83
  183.6 2.9 %copy.28 = f32[512,1024]{1,0:T(8,128)} copy(f32[512,1024]{0,1:T(8,128)} %get-tuple-element.48) | data formatting | bytes 4194304 | tf_op jit(solution)/shard_map/while | solution.py:86
  186.5 31.1 %all_to_all.29 = f32[8,64,1024]{2,1,0:T(8,128)S(1)} all-to-all(f32[8,64,1024]{2,1,0:T(8,128)} %bitcast.86), channel_id=1, replica_groups=mesh['req'=16,'ctx'=8] {'ctx'}, dimensions={0} | all-to-all | bytes 4194304 | tf_op jit(solution)/shard_map/all_to_all | solution.py:35
  (46 shorter events, 24.6 us)
Async XLA Ops:
  0.0 218.1 %copy-start = (bf16[1024,1024]{1,0:T(8,128)(2,1)S(1)}, bf16[1024,1024]{1,0:T(8,128)(2,1)}, u32[]{:S(2)}) copy-start(bf16[1024,1024]{1,0:T(8,128)(2,1)} %param.16) | copy-start | bytes 6291460
  38.0 0.7 copy-start.1
  39.9 31.4 %all-to-all-start.2 = ((bf16[8,64,1024]{2,1,0:T(8,128)(2,1)}), bf16[8,64,1024]{2,1,0:T(8,128)(2,1)S(1)}, u32[]{:S(2)}, u32[]{:S(2)}) async-start(bf16[8,64,1024]{2,1,0:T(8,128)(2,1)} %broadcast_in_dim.15), calls=%async_computation.2 | async-start | bytes 2097152 | tf_op jit(solution)/shard_map/all_to_all | solution.py:11
  186.5 31.6 %copy-start.2 = (bf16[64,2048]{1,0:T(8,128)(2,1)S(1)}, bf16[64,2048]{1,0:T(8,128)(2,1)}, u32[]{:S(2)}) copy-start(bf16[64,2048]{1,0:T(8,128)(2,1)} %copy-done.1) | copy-start | bytes 786436
where the time goes:
time: 220 us; the launch traced here: 219 us
  local copies, waits for them, and re-layouts  60.5 us (28%)
  matrix products  56.1 us (26%)
  blocking collectives  55 us (25%)
  other arithmetic  39 us (18%)
  starting transfers between devices  8 us (4%)
    dot_general x8, matrix products, step(): jnp.einsum('hqk,khd->qhd', weights, value_block, preferred_element_type=j...  50.4 us
    add x8, other arithmetic, step(): return running + added.reshape(row_count, width)  31.9 us
    all_to_all x1, blocking collectives, summed_on_arrival(): parts = lax.all_to_all(split_up(shard, dim, size), axis, 0, 0, tiled=True)  31.1 us
    unnamed x9, local copies, waits for them, and re-layouts  23.7 us
    dynamic_slice x8, local copies, waits for them, and re-layouts, step(): lax.dynamic_slice_in_dim(keys_local, start, block_keys, 0)  21.6 us
    all_to_all x1, blocking collectives, fetch_rows(): lax.all_to_all(outgoing, 'req', split_axis=0, concat_axis=0, tiled=True)  14.6 us
    all_to_all x1, blocking collectives, fetch_rows(): lax.all_to_all(looked_up, 'req', split_axis=0, concat_axis=0, tiled=True)  9.22 us
    all_to_all x1, starting transfers between devices, from_everyone(): lax.all_to_all(jnp.broadcast_to(shard[None], (size, *shard.shape)), axis,...  8 us
  transfers between devices with their start and end apart: 1, of which 0 were waited for; matrix products, arithmetic and copies ran while one was open for 10% of the time, Pallas kernels for 0%

commit v1 on v0

v1 whole, which is shorter than its diff:
```python
import jax
import jax.numpy as jnp
from jax import lax
from jax.experimental import pallas as pl
from jax.experimental.pallas import tpu as pltpu
from jax.sharding import PartitionSpec as P

MESH = pl.DeviceIdType.MESH
F32, BF16, I32 = jnp.float32, jnp.bfloat16, jnp.int32
HEADS, DH, WIDTH = 8, 128, 1024
OWNERS, CAP = 16, 8
HALF = 64
PAIR = 2 * HALF
KEYS = 4096
ITEMS = 2048
DE = 256
QSCALE = 0.5 * DH ** (-0.5)


def silu(values):
    half = 0.5 * values
    return half + half * jnp.tanh(half)


def layer_norm(values):
    centre = jnp.mean(values, axis=-1, keepdims=True)
    centred = values - centre
    spread = jnp.mean(centred * centred, axis=-1, keepdims=True)
    return centred * lax.rsqrt(spread + 1e-05)


def ranked_hits(named, wanted):
    shape = (2 * PAIR, PAIR)
    row = lax.broadcasted_iota(I32, shape, 0)
    lane = lax.broadcasted_iota(I32, shape, 1)
    half = lax.rem(lax.div(row, CAP), 2)
    place = lax.rem(row, CAP)
    match = jnp.where((named == wanted) & (lax.div(lane, HALF) == half), 1.0, 0.0)
    upto = jnp.where(
        lax.broadcasted_iota(I32, (PAIR, PAIR), 0) <= lax.broadcasted_iota(I32, (PAIR, PAIR), 1),
        1.0,
        0.0,
    ).astype(BF16)
    rank = jnp.dot(match.astype(BF16), upto, preferred_element_type=F32)
    return jnp.where(rank == (place + 1).astype(F32), match, 0.0)


def kernel(
    owner_ref, slot_ref, len_ref, table_hbm, w_in_hbm, w_uq_hbm, w_out_hbm, k_hbm, v_hbm,
    out_ref,
    owners, slots, table, w_in, w_uq, w_out, keys, vals, rowbuf, got, emb, feat, norm, query,
    acc, own, sbuf, relay, parts,
    load_sem, kv_sem, id_send, id_recv, row_send, row_recv, emb_send, emb_recv,
    part_send, relay_recv, part_recv,
):
    req = lax.axis_index("req")
    ctx = lax.axis_index("ctx")
    y, core = lax.div(ctx, 2), lax.rem(ctx, 2)
    up, down, far = lax.rem(y + 1, 4), lax.rem(y + 3, 4), lax.rem(y + 2, 4)
    partner = y * 2 + 1 - core

    loads = [
        pltpu.make_async_copy(src, dst, load_sem.at[n])
        for n, (src, dst) in enumerate(
            [(table_hbm, table), (w_in_hbm, w_in), (w_uq_hbm, w_uq), (w_out_hbm, w_out)]
        )
    ]

    def kv_copy(which, head):
        src, dst = ((k_hbm, keys), (v_hbm, vals))[which]
        return pltpu.make_async_copy(
            src.at[0, :, pl.ds(pl.multiple_of(head * DH, DH), DH)], dst.at[head], kv_sem.at[which, head]
        )

    barrier = pltpu.get_barrier_semaphore()

    def greet(step, carry):
        pl.semaphore_signal(
            barrier, inc=1, device_id=(lax.rem(req + step, OWNERS), ctx), device_id_type=MESH
        )
        return carry

    lax.fori_loop(1, OWNERS, greet, 0)
    for other in (partner, up * 2, up * 2 + 1, down * 2, down * 2 + 1, far * 2 + core):
        pl.semaphore_signal(barrier, inc=1, device_id=(req, other), device_id_type=MESH)
    for load in loads:
        load.start()
    lanes = pl.ds(pl.multiple_of(y * PAIR, PAIR), PAIR)
    own_ids = [
        pltpu.make_async_copy(owner_ref.at[:, lanes], owners.at[req], id_recv.at[0, req]),
        pltpu.make_async_copy(slot_ref.at[:, lanes], slots.at[req], id_recv.at[1, req]),
    ]
    for copy in own_ids:
        copy.start()
    pl.semaphore_wait(barrier, OWNERS - 1 + 6)

    def id_copy(which, peer, index):
        src, dst = ((owner_ref, owners), (slot_ref, slots))[which]
        return pltpu.make_async_remote_copy(
            src_ref=src.at[:, lanes],
            dst_ref=dst.at[index],
            send_sem=id_send.at[which, peer],
            recv_sem=id_recv.at[which, index],
            device_id=(peer, ctx),
            device_id_type=MESH,
        )

    def send_ids(step, carry):
        peer = lax.rem(req + step, OWNERS)
        id_copy(0, peer, req).start()
        id_copy(1, peer, req).start()
        return carry

    lax.fori_loop(1, OWNERS, send_ids, 0)

    def start_kv(head, carry):
        kv_copy(0, head).start()
        kv_copy(1, head).start()
        return carry

    lax.fori_loop(0, HEADS, start_kv, 0)
    loads[0].wait()
    for copy in own_ids:
        copy.wait()

    def wait_ids(step, carry):
        peer = lax.rem(req + step, OWNERS)
        for which in range(2):
            copy = id_copy(which, peer, peer)
            copy.wait_recv()
        return carry

    lax.fori_loop(1, OWNERS, wait_ids, 0)

    wide = (OWNERS, 2 * CAP, PAIR)
    named = jnp.broadcast_to(owners[...], wide).reshape(2 * PAIR, PAIR)
    asked = jnp.broadcast_to(slots[...], wide).reshape(2 * PAIR, PAIR)
    hits = ranked_hits(named, req)
    chosen = jnp.sum(hits * asked.astype(F32), axis=1, keepdims=True).astype(I32)
    onehot = jnp.where(
        lax.broadcasted_iota(I32, (2 * PAIR, ITEMS), 1) == chosen, 1.0, 0.0
    ).astype(BF16)
    rows = jnp.dot(onehot, table[...], preferred_element_type=F32)
    rowbuf[...] = rows.reshape(OWNERS, 2 * CAP, DE).astype(BF16)

    def row_copy(peer, index):
        return pltpu.make_async_remote_copy(
            src_ref=rowbuf.at[peer],
            dst_ref=got.at[index],
            send_sem=row_send.at[peer],
            recv_sem=row_recv.at[index],
            device_id=(peer, ctx),
            device_id_type=MESH,
        )

    def send_rows(step, carry):
        row_copy(lax.rem(req + step, OWNERS), req).start()
        return carry

    lax.fori_loop(1, OWNERS, send_rows, 0)
    got[req] = rowbuf[req]

    mine = jnp.broadcast_to(owners[req], (2 * PAIR, PAIR))
    giver = lax.div(lax.broadcasted_iota(I32, (2 * PAIR, PAIR), 0), 2 * CAP)
    order = jnp.transpose(ranked_hits(mine, giver)).astype(BF16)

    def wait_kv(head, carry):
        kv_copy(0, head).wait()
        kv_copy(1, head).wait()
        return carry

    lax.fori_loop(0, HEADS, wait_kv, 0)
    live = len_ref[0] - ctx * KEYS
    chunk = 256

    def cut(step, carry):
        start = pl.multiple_of(step * chunk, chunk)
        place = lax.broadcasted_iota(I32, (chunk, DH), 0) + start
        keep = jnp.where(place < live, 1.0, 0.0).astype(BF16)
        for head in range(HEADS):
            vals[head, pl.ds(start, chunk), :] = vals[head, pl.ds(start, chunk), :] * keep
        return carry

    lax.fori_loop(0, KEYS // chunk, cut, 0)
    for load in loads[1:]:
        load.wait()

    def wait_rows(step, carry):
        peer = lax.rem(req + step, OWNERS)
        row_copy(peer, peer).wait_recv()
        return carry

    lax.fori_loop(1, OWNERS, wait_rows, 0)
    emb[0] = jnp.dot(
        order, got[...].reshape(2 * PAIR, DE), preferred_element_type=F32
    ).astype(BF16)

    def emb_copy(block, chip):
        return pltpu.make_async_remote_copy(
            src_ref=emb.at[0],
            dst_ref=emb.at[block],
            send_sem=emb_send.at[block],
            recv_sem=emb_recv.at[block],
            device_id=(req, chip * 2 + core),
            device_id_type=MESH,
        )

    emb_copies = [emb_copy(1, far), emb_copy(2, down), emb_copy(3, up)]
    for copy in emb_copies:
        copy.start()

    def project(block):
        features = jnp.dot(emb[block], w_in[...], preferred_element_type=F32).astype(BF16)
        normed = layer_norm(features.astype(F32)).astype(BF16)
        raw = jnp.dot(normed, w_uq[:, WIDTH:], preferred_element_type=F32)
        scaled = (silu(raw) * QSCALE).astype(BF16)
        for head in range(HEADS):
            query[min(block, 1), head] = scaled[:, head * DH : (head + 1) * DH]
        return features, normed

    def relay_copy(part):
        heads = pl.ds(part * 4, 4)
        return pltpu.make_async_remote_copy(
            src_ref=sbuf.at[1, heads],
            dst_ref=relay.at[heads],
            send_sem=part_send.at[1, part, 0],
            recv_sem=relay_recv.at[part],
            device_id=(req, up * 2 + core),
            device_id_type=MESH,
        )

    def part_copy(block, part, side, chip, slot):
        heads = pl.ds(part * 4, 4)
        rows_there = pl.ds(pl.multiple_of(side * HALF, HALF), HALF)
        return pltpu.make_async_remote_copy(
            src_ref=sbuf.at[block, heads, rows_there],
            dst_ref=parts.at[slot, heads],
            send_sem=part_send.at[block, part, 0 if block == 0 else side],
            recv_sem=part_recv.at[slot, part],
            device_id=(req, chip * 2 + side),
            device_id_type=MESH,
        )

    def step(index, carry):
        block = lax.rem(lax.div(index + 1, 2), 4)
        part = jnp.where(index == 7, 1, jnp.where(index == 0, 0, lax.rem(index + 1, 2)))

        @pl.when(index == 0)
        def _():
            features, normed = project(0)
            feat[...] = features
            norm[...] = normed

        for number, copy in enumerate(emb_copies):

            @pl.when(index == 2 * number + 1)
            def _():
                copy.wait_recv()
                project(number + 1)

        for head in range(4):
            at = part * 4 + head
            score = lax.dot_general(
                query[jnp.minimum(block, 1), at], keys[at], (((1,), (1,)), ((), ())), preferred_element_type=F32
            )
            weight = (score + score * jnp.tanh(score)).astype(BF16)
            acc[head] = jnp.dot(weight, vals[at], preferred_element_type=F32)

        heads = pl.ds(part * 4, 4)

        @pl.when(block == 0)
        def _():
            sbuf[0, heads] = acc[...].astype(BF16)
            own[heads] = acc[:, pl.ds(pl.multiple_of(core * HALF, HALF), HALF), :]
            part_copy(0, part, 1 - core, y, 4).start()

        @pl.when(block == 1)
        def _():
            sbuf[1, heads] = acc[...].astype(BF16)
            relay_copy(part).start()

        @pl.when(block == 2)
        def _():
            relay_copy(part).wait_recv()
            sbuf[2, heads] = (acc[...] + relay[heads].astype(F32)).astype(BF16)
            for side in range(2):
                part_copy(2, part, side, up, core).start()

        @pl.when(block == 3)
        def _():
            sbuf[3, heads] = acc[...].astype(BF16)
            for side in range(2):
                part_copy(3, part, side, down, 2 + core).start()

        return carry

    lax.fori_loop(0, 8, step, 0)

    my_rows = pl.ds(pl.multiple_of(core * HALF, HALF), HALF)
    gate = silu(
        jnp.dot(norm[my_rows, :], w_uq[:, :WIDTH], preferred_element_type=F32)
    ).astype(BF16)
    for part in range(2):
        for slot in range(5):
            part_copy(0, part, 1 - core, y, slot).wait_recv()
    total = own[...]
    for slot in range(5):
        total = total + parts[slot].astype(F32)
    attended = jnp.concatenate([total[head] for head in range(HEADS)], axis=-1)
    mixed = (layer_norm(attended) * gate.astype(F32)).astype(BF16)
    ranked = feat[my_rows, :].astype(F32) + jnp.dot(
        mixed, w_out[...], preferred_element_type=F32
    )
    out_ref[...] = ranked.astype(BF16)

    def drain(step, carry):
        peer = lax.rem(req + step, OWNERS)
        id_copy(0, peer, req).wait_send()
        id_copy(1, peer, req).wait_send()
        row_copy(peer, req).wait_send()
        return carry

    lax.fori_loop(1, OWNERS, drain, 0)
    for copy in emb_copies:
        copy.wait_send()
    for part in range(2):
        part_copy(0, part, 1 - core, y, 4).wait_send()
        relay_copy(part).wait_send()
        for side in range(2):
            part_copy(2, part, side, up, core).wait_send()
            part_copy(3, part, side, down, 2 + core).wait_send()


def shards(item_table, cand_owner, cand_slot, w_in, w_uq, w_out, k_cache, v_cache, hist_len):
    hbm = pl.BlockSpec(memory_space=pl.ANY)
    vmem = pl.BlockSpec(memory_space=pltpu.VMEM)
    smem = pl.BlockSpec(memory_space=pltpu.SMEM)
    dma = pltpu.SemaphoreType.DMA
    out = pl.pallas_call(
        kernel,
        out_shape=jax.ShapeDtypeStruct((HALF, WIDTH), BF16),
        in_specs=[vmem, vmem, smem] + [hbm] * 6,
        out_specs=vmem,
        scratch_shapes=[
            pltpu.VMEM((OWNERS, 1, PAIR), I32),
            pltpu.VMEM((OWNERS, 1, PAIR), I32),
            pltpu.VMEM((ITEMS, DE), BF16),
            pltpu.VMEM((DE, WIDTH), BF16),
            pltpu.VMEM((WIDTH, 2 * WIDTH), BF16),
            pltpu.VMEM((WIDTH, WIDTH), BF16),
            pltpu.VMEM((HEADS, KEYS, DH), BF16),
            pltpu.VMEM((HEADS, KEYS, DH), BF16),
            pltpu.VMEM((OWNERS, 2 * CAP, DE), BF16),
            pltpu.VMEM((OWNERS, 2 * CAP, DE), BF16),
            pltpu.VMEM((4, PAIR, DE), BF16),
            pltpu.VMEM((PAIR, WIDTH), BF16),
            pltpu.VMEM((PAIR, WIDTH), BF16),
            pltpu.VMEM((2, HEADS, PAIR, DH), BF16),
            pltpu.VMEM((4, PAIR, DH), F32),
            pltpu.VMEM((HEADS, HALF, DH), F32),
            pltpu.VMEM((4, HEADS, PAIR, DH), BF16),
            pltpu.VMEM((HEADS, PAIR, DH), BF16),
            pltpu.VMEM((5, HEADS, HALF, DH), BF16),
            dma((4,)),
            dma((2, HEADS)),
            dma((2, OWNERS)),
            dma((2, OWNERS)),
            dma((OWNERS,)),
            dma((OWNERS,)),
            dma((4,)),
            dma((4,)),
            dma((4, 2, 2)),
            dma((2,)),
            dma((5, 2)),
        ],
        compiler_params=pltpu.CompilerParams(
            collective_id=0, has_side_effects=True, vmem_limit_bytes=56 * 2**20
        ),
    )(
        cand_owner.reshape(1, cand_owner.shape[1]),
        cand_slot,
        hist_len,
        item_table,
        w_in,
        w_uq,
        w_out,
        k_cache,
        v_cache,
    )
    return out[None]


def solution(mesh):
    in_specs = (
        P("req", None),
        P("req", None, None),
        P("req", None),
        P(),
        P(),
        P(),
        P("req", "ctx", None),
        P("req", "ctx", None),
        P("req"),
    )
    out_specs = P("req", "ctx", None)
    return jax.shard_map(shards, mesh=mesh, in_specs=in_specs, out_specs=out_specs, check_vma=False)
```

time: 220 us -> 50.3 us (0.23)
  local copies, waits for them, and re-layouts: 60.5 us -> 1.57 us
  matrix products: 56.1 us -> 0 us
  blocking collectives: 55 us -> 0 us
  Pallas kernels: 0 us -> 48 us
  other arithmetic: 39 us -> 0 us
  starting transfers between devices: 8 us -> 0 us
    dot_general x11 -> x0, matrix products: 56.1 us -> none  [the longest x8 50.4 us: step(): jnp.einsum('hqk,khd->qhd', weights, value_block, preferred_element_type=j...]
    all_to_all x3 -> x0, blocking collectives: 55 us -> none  [the longest x1 31.1 us: summed_on_arrival(): parts = lax.all_to_all(split_up(shard, dim, size), axis, 0, 0, tiled=True)]
    pallas_call x0 -> x1, Pallas kernels: none -> 48 us  [shards(): pl.pallas_call(kernel, out_shape=jax.ShapeDtypeStruct((HALF, WIDTH), BF16...]
    add x8 -> x0, other arithmetic: 31.9 us -> none  [step(): return running + added.reshape(row_count, width)]
    dynamic_slice x9 -> x0, local copies, waits for them, and re-layouts: 22.4 us -> none  [the longest x8 21.6 us: step(): lax.dynamic_slice_in_dim(keys_local, start, block_keys, 0)]
    unnamed x9 -> x1, local copies, waits for them, and re-layouts: 23.7 us -> 1.57 us
    all_to_all x1 -> x0, starting transfers between devices: 8 us -> none  [from_everyone(): lax.all_to_all(jnp.broadcast_to(shard[None], (size, *shard.shape)), axis,...]
    lt x8 -> x0, other arithmetic: 5.2 us -> none  [step(): position[None, None, :] < length]
  transfers between devices with their start and end apart: 1 -> 0, of which waited for: 0 -> 0; matrix products, arithmetic and copies ran while one was open for 10% -> 0% of each run, Pallas kernels for 0% -> 0%
where the time goes in v1:
time: 50.3 us; the launch traced here: 50.2 us
  Pallas kernels  48 us (95%)
  local copies, waits for them, and re-layouts  1.57 us (3%)
  between operations  0.66 us (1%)
    pallas_call x1, Pallas kernels, shards(): pl.pallas_call(kernel, out_shape=jax.ShapeDtypeStruct((HALF, WIDTH), BF16...  48 us
    unnamed x1, local copies, waits for them, and re-layouts  1.57 us

profile of v1, /device:TPU:1, one launch (start us, length us, event | category | flops | bytes accessed | tf_op | source)
XLA Modules:
  0.0 50.2 jit_solution(1062340957991966001)
XLA Ops:
  0.7 48.0 %shard_map.91 = bf16[64,1024]{1,0:T(8,128)(2,1)} custom-call(s32[1,512]{1,0:T(1,128)} %bitcast.3, s32[1,512]{1,0:T(1,128)} %slot_ref.1, s32[1]{0:T(128)S(6)} %copy.11.len_ref, bf16[2048,256]{1,0:T(8,128)(2,1)} %table_hbm.1, bf16[256,1024]{1,0:T(8,128)(2,1)} %w_in_hbm.1, bf16[1024,2048]{1,0:T(8,128)(2,1)} %w_uq_hbm.1, bf16[1024,1024]{1,0:T(8,128)(2,1)} %w_out_hbm.1, ...), custom_call_target="tpu_custom_call" | custom-call | tf_op jit(solution)/shard_map/pallas_call | solution.py:339
  48.6 1.6 %copy.12 = bf16[1,64,1024]{2,1,0:T(8,128)(2,1)} copy(bf16[1,64,1024]{2,1,0:T(8,128)(2,1)} %bitcast.2) | data formatting | bytes 262144

commit v2 on v1

--- a/solution.py
+++ b/solution.py
@@ -46,12 +46,12 @@
 
 
 def kernel(
-    owner_ref, slot_ref, len_ref, table_hbm, w_in_hbm, w_uq_hbm, w_out_hbm, k_hbm, v_hbm,
+    owner_hbm, slot_hbm, len_ref, table_hbm, w_in_hbm, w_uq_hbm, w_out_hbm, k_hbm, v_hbm,
     out_ref,
     owners, slots, table, w_in, w_uq, w_out, keys, vals, rowbuf, got, emb, feat, norm, query,
-    acc, own, sbuf, relay, parts,
+    query_wide, acc, mine, theirs, swapped, sums, parts,
     load_sem, kv_sem, id_send, id_recv, row_send, row_recv, emb_send, emb_recv,
-    part_send, relay_recv, part_recv,
+    swap_send, swap_recv, part_send, part_recv,
 ):
     req = lax.axis_index("req")
     ctx = lax.axis_index("ctx")
@@ -81,24 +81,24 @@
         return carry
 
     lax.fori_loop(1, OWNERS, greet, 0)
-    for other in (partner, up * 2, up * 2 + 1, down * 2, down * 2 + 1, far * 2 + core):
+    for other in (partner, up * 2 + core, down * 2 + core, far * 2 + core):
         pl.semaphore_signal(barrier, inc=1, device_id=(req, other), device_id_type=MESH)
-    for load in loads:
-        load.start()
     lanes = pl.ds(pl.multiple_of(y * PAIR, PAIR), PAIR)
     own_ids = [
-        pltpu.make_async_copy(owner_ref.at[:, lanes], owners.at[req], id_recv.at[0, req]),
-        pltpu.make_async_copy(slot_ref.at[:, lanes], slots.at[req], id_recv.at[1, req]),
+        pltpu.make_async_copy(owner_hbm.at[:, lanes], owners.at[req], id_recv.at[0, req]),
+        pltpu.make_async_copy(slot_hbm.at[:, lanes], slots.at[req], id_recv.at[1, req]),
     ]
+    for copy in [*own_ids, *loads]:
+        copy.start()
     for copy in own_ids:
-        copy.start()
-    pl.semaphore_wait(barrier, OWNERS - 1 + 6)
+        copy.wait()
+    pl.semaphore_wait(barrier, OWNERS - 1 + 4)
 
     def id_copy(which, peer, index):
-        src, dst = ((owner_ref, owners), (slot_ref, slots))[which]
+        ids = (owners, slots)[which]
         return pltpu.make_async_remote_copy(
-            src_ref=src.at[:, lanes],
-            dst_ref=dst.at[index],
+            src_ref=ids.at[req],
+            dst_ref=ids.at[index],
             send_sem=id_send.at[which, peer],
             recv_sem=id_recv.at[which, index],
             device_id=(peer, ctx),
@@ -120,8 +120,6 @@
 
     lax.fori_loop(0, HEADS, start_kv, 0)
     loads[0].wait()
-    for copy in own_ids:
-        copy.wait()
 
     def wait_ids(step, carry):
         peer = lax.rem(req + step, OWNERS)
@@ -160,9 +158,9 @@
     lax.fori_loop(1, OWNERS, send_rows, 0)
     got[req] = rowbuf[req]
 
-    mine = jnp.broadcast_to(owners[req], (2 * PAIR, PAIR))
+    asked_here = jnp.broadcast_to(owners[req], (2 * PAIR, PAIR))
     giver = lax.div(lax.broadcasted_iota(I32, (2 * PAIR, PAIR), 0), 2 * CAP)
-    order = jnp.transpose(ranked_hits(mine, giver)).astype(BF16)
+    order = jnp.transpose(ranked_hits(asked_here, giver)).astype(BF16)
 
     def wait_kv(head, carry):
         kv_copy(0, head).wait()
@@ -209,103 +207,151 @@
     for copy in emb_copies:
         copy.start()
 
-    def project(block):
-        features = jnp.dot(emb[block], w_in[...], preferred_element_type=F32).astype(BF16)
+    def project(rows_in):
+        features = jnp.dot(rows_in, w_in[...], preferred_element_type=F32).astype(BF16)
         normed = layer_norm(features.astype(F32)).astype(BF16)
         raw = jnp.dot(normed, w_uq[:, WIDTH:], preferred_element_type=F32)
-        scaled = (silu(raw) * QSCALE).astype(BF16)
+        return features, normed, (silu(raw) * QSCALE).astype(BF16)
+
+    def keep_query(buffer, scaled):
         for head in range(HEADS):
-            query[min(block, 1), head] = scaled[:, head * DH : (head + 1) * DH]
-        return features, normed
-
-    def relay_copy(part):
-        heads = pl.ds(part * 4, 4)
+            buffer[head] = scaled[:, head * DH : (head + 1) * DH]
+
+    my_rows = pl.ds(pl.multiple_of(core * HALF, HALF), HALF)
+    their_rows = pl.ds(pl.multiple_of((1 - core) * HALF, HALF), HALF)
+
+    def swap_copy(block, pair):
+        heads = pl.ds(pair * 2, 2)
         return pltpu.make_async_remote_copy(
-            src_ref=sbuf.at[1, heads],
-            dst_ref=relay.at[heads],
-            send_sem=part_send.at[1, part, 0],
-            recv_sem=relay_recv.at[part],
-            device_id=(req, up * 2 + core),
+            src_ref=theirs.at[block, heads],
+            dst_ref=swapped.at[block, heads],
+            send_sem=swap_send.at[block, pair],
+            recv_sem=swap_recv.at[block, pair],
+            device_id=(req, partner),
             device_id_type=MESH,
         )
 
-    def part_copy(block, part, side, chip, slot):
-        heads = pl.ds(part * 4, 4)
-        rows_there = pl.ds(pl.multiple_of(side * HALF, HALF), HALF)
+    def hand_over(block, pair, first):
+        heads = pl.ds(pair * 2, 2)
+        mine[block, heads] = acc[first : first + 2, my_rows, :]
+        theirs[block, heads] = acc[first : first + 2, their_rows, :].astype(BF16)
+        swap_copy(block, pair).start()
+
+    def sum_copy(block, pair):
+        heads = pl.ds(pair * 2, 2)
         return pltpu.make_async_remote_copy(
-            src_ref=sbuf.at[block, heads, rows_there],
-            dst_ref=parts.at[slot, heads],
-            send_sem=part_send.at[block, part, 0 if block == 0 else side],
-            recv_sem=part_recv.at[slot, part],
-            device_id=(req, chip * 2 + side),
+            src_ref=sums.at[block, heads],
+            dst_ref=parts.at[block, heads],
+            send_sem=part_send.at[block, pair],
+            recv_sem=part_recv.at[block, pair],
+            device_id=(req, (y, far, up, down)[block] * 2 + core),
             device_id_type=MESH,
         )
 
-    def step(index, carry):
-        block = lax.rem(lax.div(index + 1, 2), 4)
-        part = jnp.where(index == 7, 1, jnp.where(index == 0, 0, lax.rem(index + 1, 2)))
+    def finish(block, pair):
+        heads = pl.ds(pair * 2, 2)
+        swap_copy(block, pair).wait_recv()
+        sums[block, heads] = (mine[block, heads] + swapped[block, heads].astype(F32)).astype(BF16)
+        sum_copy(block, pair).start()
+
+    def attend(asking, head):
+        score = lax.dot_general(
+            asking, keys[head], (((1,), (1,)), ((), ())), preferred_element_type=F32
+        )
+        weight = (score + score * jnp.tanh(score)).astype(BF16)
+        return jnp.dot(weight, vals[head], preferred_element_type=F32)
+
+    features, normed, scaled = project(emb[0])
+    feat[...] = features
+    norm[...] = normed
+    keep_query(query.at[0], scaled)
+    for head in range(4):
+        acc[head] = attend(query[0, head], head)
+    for pair in range(2):
+        hand_over(0, pair, 2 * pair)
+
+    for copy in emb_copies[:2]:
+        copy.wait_recv()
+    keep_query(query_wide, project(emb[1:3].reshape(2 * PAIR, DE))[2])
+    piece = 512
+    pieces = KEYS // piece
+
+    def wide_step(pair, carry):
+        def scored(item):
+            head = pair * 2 + item // pieces
+            start = (item % pieces) * piece
+            return lax.dot_general(
+                keys[head, start : start + piece, :],
+                query_wide[head],
+                (((1,), (1,)), ((), ())),
+                preferred_element_type=F32,
+            )
+
+        score = scored(0)
+        total = None
+        for item in range(2 * pieces):
+            ahead = scored(item + 1) if item + 1 < 2 * pieces else None
+            weight = (score + score * jnp.tanh(score)).astype(BF16)
+            start = (item % pieces) * piece
+            added = lax.dot_general(
+                vals[pair * 2 + item // pieces, start : start + piece, :],
+                weight,
+                (((0,), (0,)), ((), ())),
+                preferred_element_type=F32,
+            )
+            total = added if item % pieces == 0 else total + added
+            if item % pieces == pieces - 1:
+                turned = jnp.transpose(total)
+                acc[item // pieces] = turned[:PAIR]
+                acc[2 + item // pieces] = turned[PAIR:]
+            score = ahead
+        hand_over(1, pair, 0)
+        hand_over(2, pair, 2)
+
+        @pl.when(pair > 0)
+        def _():
+            finish(1, pair - 1)
+            finish(2, pair - 1)
+
+        return carry
+
+    lax.fori_loop(0, 4, wide_step, 0)
+
+    emb_copies[2].wait_recv()
+    keep_query(query.at[1], project(emb[3])[2])
+
+    def last_step(index, carry):
+        other = index < 4
+        block = jnp.where(other, 3, 0)
+        pair = jnp.where(other, index, index - 2)
+        which = jnp.where(other, 1, 0)
+        for head in range(2):
+            acc[head] = attend(query[which, pair * 2 + head], pair * 2 + head)
+        hand_over(block, pair, 0)
 
         @pl.when(index == 0)
         def _():
-            features, normed = project(0)
-            feat[...] = features
-            norm[...] = normed
-
-        for number, copy in enumerate(emb_copies):
-
-            @pl.when(index == 2 * number + 1)
-            def _():
-                copy.wait_recv()
-                project(number + 1)
-
-        for head in range(4):
-            at = part * 4 + head
-            score = lax.dot_general(
-                query[jnp.minimum(block, 1), at], keys[at], (((1,), (1,)), ((), ())), preferred_element_type=F32
-            )
-            weight = (score + score * jnp.tanh(score)).astype(BF16)
-            acc[head] = jnp.dot(weight, vals[at], preferred_element_type=F32)
-
-        heads = pl.ds(part * 4, 4)
-
-        @pl.when(block == 0)
+            finish(1, 3)
+            finish(2, 3)
+
+        @pl.when((index > 0) & (index < 5))
         def _():
-            sbuf[0, heads] = acc[...].astype(BF16)
-            own[heads] = acc[:, pl.ds(pl.multiple_of(core * HALF, HALF), HALF), :]
-            part_copy(0, part, 1 - core, y, 4).start()
-
-        @pl.when(block == 1)
-        def _():
-            sbuf[1, heads] = acc[...].astype(BF16)
-            relay_copy(part).start()
-
-        @pl.when(block == 2)
-        def _():
-            relay_copy(part).wait_recv()
-            sbuf[2, heads] = (acc[...] + relay[heads].astype(F32)).astype(BF16)
-            for side in range(2):
-                part_copy(2, part, side, up, core).start()
-
-        @pl.when(block == 3)
-        def _():
-            sbuf[3, heads] = acc[...].astype(BF16)
-            for side in range(2):
-                part_copy(3, part, side, down, 2 + core).start()
-
-        return carry
-
-    lax.fori_loop(0, 8, step, 0)
-
-    my_rows = pl.ds(pl.multiple_of(core * HALF, HALF), HALF)
+            finish(3, index - 1)
+
+        return carry
+
+    lax.fori_loop(0, 6, last_step, 0)
+
     gate = silu(
         jnp.dot(norm[my_rows, :], w_uq[:, :WIDTH], preferred_element_type=F32)
     ).astype(BF16)
-    for part in range(2):
-        for slot in range(5):
-            part_copy(0, part, 1 - core, y, slot).wait_recv()
-    total = own[...]
-    for slot in range(5):
-        total = total + parts[slot].astype(F32)
+    for pair in range(4):
+        swap_copy(0, pair).wait_recv()
+        for block in range(1, 4):
+            sum_copy(block, pair).wait_recv()
+    total = mine[0] + swapped[0].astype(F32)
+    for block in range(1, 4):
+        total = total + parts[block].astype(F32)
     attended = jnp.concatenate([total[head] for head in range(HEADS)], axis=-1)
     mixed = (layer_norm(attended) * gate.astype(F32)).astype(BF16)
     ranked = feat[my_rows, :].astype(F32) + jnp.dot(
@@ -323,23 +369,21 @@
     lax.fori_loop(1, OWNERS, drain, 0)
     for copy in emb_copies:
         copy.wait_send()
-    for part in range(2):
-        part_copy(0, part, 1 - core, y, 4).wait_send()
-        relay_copy(part).wait_send()
-        for side in range(2):
-            part_copy(2, part, side, up, core).wait_send()
-            part_copy(3, part, side, down, 2 + core).wait_send()
+    for pair in range(4):
+        for block in range(4):
+            swap_copy(block, pair).wait_send()
+        for block in range(1, 4):
+            sum_copy(block, pair).wait_send()
 
 
 def shards(item_table, cand_owner, cand_slot, w_in, w_uq, w_out, k_cache, v_cache, hist_len):
     hbm = pl.BlockSpec(memory_space=pl.ANY)
     vmem = pl.BlockSpec(memory_space=pltpu.VMEM)
-    smem = pl.BlockSpec(memory_space=pltpu.SMEM)
     dma = pltpu.SemaphoreType.DMA
     out = pl.pallas_call(
         kernel,
-        out_shape=jax.ShapeDtypeStruct((HALF, WIDTH), BF16),
-        in_specs=[vmem, vmem, smem] + [hbm] * 6,
+        out_shape=pltpu.VMEM((HALF, WIDTH), BF16),
+        in_specs=[hbm, hbm, pl.BlockSpec(memory_space=pltpu.SMEM)] + [hbm] * 6,
         out_specs=vmem,
         scratch_shapes=[
             pltpu.VMEM((OWNERS, 1, PAIR), I32),
@@ -356,11 +400,13 @@
             pltpu.VMEM((PAIR, WIDTH), BF16),
             pltpu.VMEM((PAIR, WIDTH), BF16),
             pltpu.VMEM((2, HEADS, PAIR, DH), BF16),
+            pltpu.VMEM((HEADS, 2 * PAIR, DH), BF16),
             pltpu.VMEM((4, PAIR, DH), F32),
-            pltpu.VMEM((HEADS, HALF, DH), F32),
-            pltpu.VMEM((4, HEADS, PAIR, DH), BF16),
-            pltpu.VMEM((HEADS, PAIR, DH), BF16),
-            pltpu.VMEM((5, HEADS, HALF, DH), BF16),
+            pltpu.VMEM((4, HEADS, HALF, DH), F32),
+            pltpu.VMEM((4, HEADS, HALF, DH), BF16),
+            pltpu.VMEM((4, HEADS, HALF, DH), BF16),
+            pltpu.VMEM((4, HEADS, HALF, DH), BF16),
+            pltpu.VMEM((4, HEADS, HALF, DH), BF16),
             dma((4,)),
             dma((2, HEADS)),
             dma((2, OWNERS)),
@@ -369,9 +415,10 @@
             dma((OWNERS,)),
             dma((4,)),
             dma((4,)),
-            dma((4, 2, 2)),
-            dma((2,)),
-            dma((5, 2)),
+            dma((4, 4)),
+            dma((4, 4)),
+            dma((4, 4)),
+            dma((4, 4)),
         ],
         compiler_params=pltpu.CompilerParams(
             collective_id=0, has_side_effects=True, vmem_limit_bytes=56 * 2**20

time: 50.3 us -> 47.5 us (0.944)
  Pallas kernels: 48 us -> 46.1 us
  local copies, waits for them, and re-layouts: 1.57 us -> 0.66 us
    pallas_call x1, Pallas kernels: 48 us -> 46.1 us  [shards(): pl.pallas_call(kernel, out_shape=pltpu.VMEM((HALF, WIDTH), BF16), in_spec...]
    unnamed x1, local copies, waits for them, and re-layouts: 1.57 us -> 0.66 us
where the time goes in v2:
time: 47.5 us; the launch traced here: 47.4 us
  Pallas kernels  46.1 us (97%)
  local copies, waits for them, and re-layouts  0.66 us (1%)
  between operations  0.66 us (1%)
    pallas_call x1, Pallas kernels, shards(): pl.pallas_call(kernel, out_shape=pltpu.VMEM((HALF, WIDTH), BF16), in_spec...  46.1 us

profile of v2, /device:TPU:1, one launch (start us, length us, event | category | flops | bytes accessed | tf_op | source)
XLA Modules:
  0.0 47.4 jit_solution(15411371269179699258)
XLA Ops:
  0.7 46.1 %shard_map.91 = bf16[64,1024]{1,0:T(8,128)(2,1)S(1)} custom-call(s32[1,512]{1,0:T(1,128)} %bitcast.3, s32[1,512]{1,0:T(1,128)} %slot_hbm.1, s32[1]{0:T(128)S(6)} %copy.12.len_ref, bf16[2048,256]{1,0:T(8,128)(2,1)} %table_hbm.1, bf16[256,1024]{1,0:T(8,128)(2,1)} %w_in_hbm.1, bf16[1024,2048]{1,0:T(8,128)(2,1)} %w_uq_hbm.1, bf16[1024,1024]{1,0:T(8,128)(2,1)} %w_out_hbm.1, ...), custom_call_target="tpu_custom_call" | custom-call | tf_op jit(solution)/shard_map/pallas_call | solution.py:383
  46.8 0.7 %copy.11 = bf16[1,64,1024]{2,1,0:T(8,128)(2,1)} copy(bf16[1,64,1024]{2,1,0:T(8,128)(2,1)S(1)} %bitcast.2) | data formatting | bytes 262144

commit v3 on v2

--- a/solution.py
+++ b/solution.py
@@ -48,9 +48,9 @@
 def kernel(
     owner_hbm, slot_hbm, len_ref, table_hbm, w_in_hbm, w_uq_hbm, w_out_hbm, k_hbm, v_hbm,
     out_ref,
-    owners, slots, table, w_in, w_uq, w_out, keys, vals, rowbuf, got, emb, feat, norm, query,
+    ids, table, w_in, w_uq, w_out, keys, vals, rowbuf, got, emb, feat, norm, query,
     query_wide, acc, mine, theirs, swapped, sums, parts,
-    load_sem, kv_sem, id_send, id_recv, row_send, row_recv, emb_send, emb_recv,
+    load_sem, kv_sem, id_load, id_send, id_recv, row_send, row_recv, emb_send, emb_recv,
     swap_send, swap_recv, part_send, part_recv,
 ):
     req = lax.axis_index("req")
@@ -74,19 +74,21 @@
 
     barrier = pltpu.get_barrier_semaphore()
 
-    def greet(step, carry):
-        pl.semaphore_signal(
-            barrier, inc=1, device_id=(lax.rem(req + step, OWNERS), ctx), device_id_type=MESH
-        )
-        return carry
-
-    lax.fori_loop(1, OWNERS, greet, 0)
+    z, x = lax.div(req, 4), lax.rem(req, 4)
+    offsets = sorted(
+        [(dz, dx) for dz in range(4) for dx in range(4) if dz or dx],
+        key=lambda way: -min(way[0], 4 - way[0]) - min(way[1], 4 - way[1]),
+    )
+    peers = [lax.rem(z + dz, 4) * 4 + lax.rem(x + dx, 4) for dz, dx in offsets]
+    for peer in peers:
+        pl.semaphore_signal(barrier, inc=1, device_id=(peer, ctx), device_id_type=MESH)
     for other in (partner, up * 2 + core, down * 2 + core, far * 2 + core):
         pl.semaphore_signal(barrier, inc=1, device_id=(req, other), device_id_type=MESH)
-    lanes = pl.ds(pl.multiple_of(y * PAIR, PAIR), PAIR)
+    asked_chip = jnp.where(core == 0, y, far)
+    lanes = pl.ds(pl.multiple_of(asked_chip * PAIR, PAIR), PAIR)
     own_ids = [
-        pltpu.make_async_copy(owner_hbm.at[:, lanes], owners.at[req], id_recv.at[0, req]),
-        pltpu.make_async_copy(slot_hbm.at[:, lanes], slots.at[req], id_recv.at[1, req]),
+        pltpu.make_async_copy(src.at[:, lanes], ids.at[req, which], id_load.at[which])
+        for which, src in enumerate((owner_hbm, slot_hbm))
     ]
     for copy in [*own_ids, *loads]:
         copy.start()
@@ -94,24 +96,18 @@
         copy.wait()
     pl.semaphore_wait(barrier, OWNERS - 1 + 4)
 
-    def id_copy(which, peer, index):
-        ids = (owners, slots)[which]
+    def id_copy(peer, index):
         return pltpu.make_async_remote_copy(
             src_ref=ids.at[req],
             dst_ref=ids.at[index],
-            send_sem=id_send.at[which, peer],
-            recv_sem=id_recv.at[which, index],
+            send_sem=id_send.at[peer],
+            recv_sem=id_recv.at[index],
             device_id=(peer, ctx),
             device_id_type=MESH,
         )
 
-    def send_ids(step, carry):
-        peer = lax.rem(req + step, OWNERS)
-        id_copy(0, peer, req).start()
-        id_copy(1, peer, req).start()
-        return carry
-
-    lax.fori_loop(1, OWNERS, send_ids, 0)
+    for peer in peers:
+        id_copy(peer, req).start()
 
     def start_kv(head, carry):
         kv_copy(0, head).start()
@@ -123,16 +119,14 @@
 
     def wait_ids(step, carry):
         peer = lax.rem(req + step, OWNERS)
-        for which in range(2):
-            copy = id_copy(which, peer, peer)
-            copy.wait_recv()
+        id_copy(peer, peer).wait_recv()
         return carry
 
     lax.fori_loop(1, OWNERS, wait_ids, 0)
 
     wide = (OWNERS, 2 * CAP, PAIR)
-    named = jnp.broadcast_to(owners[...], wide).reshape(2 * PAIR, PAIR)
-    asked = jnp.broadcast_to(slots[...], wide).reshape(2 * PAIR, PAIR)
+    named = jnp.broadcast_to(ids[:, 0], wide).reshape(2 * PAIR, PAIR)
+    asked = jnp.broadcast_to(ids[:, 1], wide).reshape(2 * PAIR, PAIR)
     hits = ranked_hits(named, req)
     chosen = jnp.sum(hits * asked.astype(F32), axis=1, keepdims=True).astype(I32)
     onehot = jnp.where(
@@ -151,14 +145,11 @@
             device_id_type=MESH,
         )
 
-    def send_rows(step, carry):
-        row_copy(lax.rem(req + step, OWNERS), req).start()
-        return carry
-
-    lax.fori_loop(1, OWNERS, send_rows, 0)
+    for peer in peers:
+        row_copy(peer, req).start()
     got[req] = rowbuf[req]
 
-    asked_here = jnp.broadcast_to(owners[req], (2 * PAIR, PAIR))
+    asked_here = jnp.broadcast_to(ids[req, 0], (2 * PAIR, PAIR))
     giver = lax.div(lax.broadcasted_iota(I32, (2 * PAIR, PAIR), 0), 2 * CAP)
     order = jnp.transpose(ranked_hits(asked_here, giver)).astype(BF16)
 
@@ -189,24 +180,22 @@
         return carry
 
     lax.fori_loop(1, OWNERS, wait_rows, 0)
-    emb[0] = jnp.dot(
+    emb[core] = jnp.dot(
         order, got[...].reshape(2 * PAIR, DE), preferred_element_type=F32
     ).astype(BF16)
 
-    def emb_copy(block, chip):
+    def emb_copy(source, block, there):
         return pltpu.make_async_remote_copy(
-            src_ref=emb.at[0],
+            src_ref=emb.at[source],
             dst_ref=emb.at[block],
             send_sem=emb_send.at[block],
             recv_sem=emb_recv.at[block],
-            device_id=(req, chip * 2 + core),
+            device_id=(req, there),
             device_id_type=MESH,
         )
 
-    emb_copies = [emb_copy(1, far), emb_copy(2, down), emb_copy(3, up)]
-    for copy in emb_copies:
-        copy.start()
-
+    emb_given = emb_copy(core, core, partner)
+    emb_given.start()
     def project(rows_in):
         features = jnp.dot(rows_in, w_in[...], preferred_element_type=F32).astype(BF16)
         normed = layer_norm(features.astype(F32)).astype(BF16)
@@ -254,35 +243,18 @@
         sums[block, heads] = (mine[block, heads] + swapped[block, heads].astype(F32)).astype(BF16)
         sum_copy(block, pair).start()
 
-    def attend(asking, head):
-        score = lax.dot_general(
-            asking, keys[head], (((1,), (1,)), ((), ())), preferred_element_type=F32
-        )
-        weight = (score + score * jnp.tanh(score)).astype(BF16)
-        return jnp.dot(weight, vals[head], preferred_element_type=F32)
-
-    features, normed, scaled = project(emb[0])
-    feat[...] = features
-    norm[...] = normed
-    keep_query(query.at[0], scaled)
-    for head in range(4):
-        acc[head] = attend(query[0, head], head)
-    for pair in range(2):
-        hand_over(0, pair, 2 * pair)
-
-    for copy in emb_copies[:2]:
-        copy.wait_recv()
-    keep_query(query_wide, project(emb[1:3].reshape(2 * PAIR, DE))[2])
+    def weigh(score):
+        return (score + score * jnp.tanh(score)).astype(BF16)
+
     piece = 512
     pieces = KEYS // piece
 
-    def wide_step(pair, carry):
+    def attend_two(pair):
         def scored(item):
-            head = pair * 2 + item // pieces
             start = (item % pieces) * piece
             return lax.dot_general(
-                keys[head, start : start + piece, :],
-                query_wide[head],
+                keys[pair * 2 + item // pieces, start : start + piece, :],
+                query_wide[pair * 2 + item // pieces],
                 (((1,), (1,)), ((), ())),
                 preferred_element_type=F32,
             )
@@ -291,11 +263,10 @@
         total = None
         for item in range(2 * pieces):
             ahead = scored(item + 1) if item + 1 < 2 * pieces else None
-            weight = (score + score * jnp.tanh(score)).astype(BF16)
             start = (item % pieces) * piece
             added = lax.dot_general(
                 vals[pair * 2 + item // pieces, start : start + piece, :],
-                weight,
+                weigh(score),
                 (((0,), (0,)), ((), ())),
                 preferred_element_type=F32,
             )
@@ -305,45 +276,77 @@
                 acc[item // pieces] = turned[:PAIR]
                 acc[2 + item // pieces] = turned[PAIR:]
             score = ahead
-        hand_over(1, pair, 0)
-        hand_over(2, pair, 2)
+        hand_over(2, pair, 0)
+        hand_over(3, pair, 2)
+
+    def attend_one(block, pair):
+        for head in range(2):
+            score = lax.dot_general(
+                query[block, pair * 2 + head],
+                keys[pair * 2 + head],
+                (((1,), (1,)), ((), ())),
+                preferred_element_type=F32,
+            )
+            acc[head] = jnp.dot(
+                weigh(score), vals[pair * 2 + head], preferred_element_type=F32
+            )
+        hand_over(block, pair, 0)
+
+    def open_block(block):
+        features, normed, scaled = project(emb[block])
+        feat[block] = features
+        norm[block] = normed
+        keep_query(query.at[block], scaled)
+        attend_one(block, 0)
+
+    open_block(core)
+    emb_copy(1 - core, 1 - core, partner).wait_recv()
+    emb_copies = [emb_copy(0, 2, down * 2 + core), emb_copy(0, 3, up * 2 + core)]
+    for copy in emb_copies:
+        copy.start()
+    open_block(1 - core)
+
+    def far_step(pair, carry):
+        attend_one(1, pair)
+        finish(1, pair - 1)
+        return carry
+
+    lax.fori_loop(1, 4, far_step, 0)
+
+    for copy in emb_copies:
+        copy.wait_recv()
+    keep_query(query_wide, project(emb[2:4].reshape(2 * PAIR, DE))[2])
+
+    def side_step(pair, carry):
+        attend_two(pair)
+
+        @pl.when(pair == 0)
+        def _():
+            finish(1, 3)
 
         @pl.when(pair > 0)
         def _():
-            finish(1, pair - 1)
             finish(2, pair - 1)
-
-        return carry
-
-    lax.fori_loop(0, 4, wide_step, 0)
-
-    emb_copies[2].wait_recv()
-    keep_query(query.at[1], project(emb[3])[2])
-
-    def last_step(index, carry):
-        other = index < 4
-        block = jnp.where(other, 3, 0)
-        pair = jnp.where(other, index, index - 2)
-        which = jnp.where(other, 1, 0)
-        for head in range(2):
-            acc[head] = attend(query[which, pair * 2 + head], pair * 2 + head)
-        hand_over(block, pair, 0)
-
-        @pl.when(index == 0)
+            finish(3, pair - 1)
+
+        return carry
+
+    lax.fori_loop(0, 4, side_step, 0)
+
+    def own_step(pair, carry):
+        attend_one(0, pair)
+
+        @pl.when(pair == 1)
         def _():
-            finish(1, 3)
             finish(2, 3)
-
-        @pl.when((index > 0) & (index < 5))
-        def _():
-            finish(3, index - 1)
-
-        return carry
-
-    lax.fori_loop(0, 6, last_step, 0)
+            finish(3, 3)
+
+        return carry
+
+    lax.fori_loop(1, 4, own_step, 0)
 
     gate = silu(
-        jnp.dot(norm[my_rows, :], w_uq[:, :WIDTH], preferred_element_type=F32)
+        jnp.dot(norm[0, my_rows, :], w_uq[:, :WIDTH], preferred_element_type=F32)
     ).astype(BF16)
     for pair in range(4):
         swap_copy(0, pair).wait_recv()
@@ -354,20 +357,19 @@
         total = total + parts[block].astype(F32)
     attended = jnp.concatenate([total[head] for head in range(HEADS)], axis=-1)
     mixed = (layer_norm(attended) * gate.astype(F32)).astype(BF16)
-    ranked = feat[my_rows, :].astype(F32) + jnp.dot(
+    ranked = feat[0, my_rows, :].astype(F32) + jnp.dot(
         mixed, w_out[...], preferred_element_type=F32
     )
     out_ref[...] = ranked.astype(BF16)
 
     def drain(step, carry):
         peer = lax.rem(req + step, OWNERS)
-        id_copy(0, peer, req).wait_send()
-        id_copy(1, peer, req).wait_send()
+        id_copy(peer, req).wait_send()
         row_copy(peer, req).wait_send()
         return carry
 
     lax.fori_loop(1, OWNERS, drain, 0)
-    for copy in emb_copies:
+    for copy in [emb_given, *emb_copies]:
         copy.wait_send()
     for pair in range(4):
         for block in range(4):
@@ -386,8 +388,7 @@
         in_specs=[hbm, hbm, pl.BlockSpec(memory_space=pltpu.SMEM)] + [hbm] * 6,
         out_specs=vmem,
         scratch_shapes=[
-            pltpu.VMEM((OWNERS, 1, PAIR), I32),
-            pltpu.VMEM((OWNERS, 1, PAIR), I32),
+            pltpu.VMEM((OWNERS, 2, 1, PAIR), I32),
             pltpu.VMEM((ITEMS, DE), BF16),
             pltpu.VMEM((DE, WIDTH), BF16),
             pltpu.VMEM((WIDTH, 2 * WIDTH), BF16),
@@ -397,8 +398,8 @@
             pltpu.VMEM((OWNERS, 2 * CAP, DE), BF16),
             pltpu.VMEM((OWNERS, 2 * CAP, DE), BF16),
             pltpu.VMEM((4, PAIR, DE), BF16),
-            pltpu.VMEM((PAIR, WIDTH), BF16),
-            pltpu.VMEM((PAIR, WIDTH), BF16),
+            pltpu.VMEM((2, PAIR, WIDTH), BF16),
+            pltpu.VMEM((2, PAIR, WIDTH), BF16),
             pltpu.VMEM((2, HEADS, PAIR, DH), BF16),
             pltpu.VMEM((HEADS, 2 * PAIR, DH), BF16),
             pltpu.VMEM((4, PAIR, DH), F32),
@@ -409,8 +410,9 @@
             pltpu.VMEM((4, HEADS, HALF, DH), BF16),
             dma((4,)),
             dma((2, HEADS)),
-            dma((2, OWNERS)),
-            dma((2, OWNERS)),
+            dma((2,)),
+            dma((OWNERS,)),
+            dma((OWNERS,)),
             dma((OWNERS,)),
             dma((OWNERS,)),
             dma((4,)),

time: 47.5 us -> 45.1 us (0.949)
  Pallas kernels: 46.1 us -> 43.6 us
    pallas_call x1, Pallas kernels: 46.1 us -> 43.6 us  [shards(): pl.pallas_call(kernel, out_shape=pltpu.VMEM((HALF, WIDTH), BF16), in_spec...]
where the time goes in v3:
time: 45.1 us; the launch traced here: 44.9 us
  Pallas kernels  43.6 us (97%)
  local copies, waits for them, and re-layouts  0.66 us (1%)
  between operations  0.66 us (1%)
    pallas_call x1, Pallas kernels, shards(): pl.pallas_call(kernel, out_shape=pltpu.VMEM((HALF, WIDTH), BF16), in_spec...  43.6 us

profile of v3, /device:TPU:1, one launch (start us, length us, event | category | flops | bytes accessed | tf_op | source)
XLA Modules:
  0.0 44.9 jit_solution(7676276008797819090)
XLA Ops:
  0.7 43.6 %shard_map.91 = bf16[64,1024]{1,0:T(8,128)(2,1)S(1)} custom-call(s32[1,512]{1,0:T(1,128)} %bitcast.3, s32[1,512]{1,0:T(1,128)} %slot_hbm.1, s32[1]{0:T(128)S(6)} %copy.12.len_ref, bf16[2048,256]{1,0:T(8,128)(2,1)} %table_hbm.1, bf16[256,1024]{1,0:T(8,128)(2,1)} %w_in_hbm.1, bf16[1024,2048]{1,0:T(8,128)(2,1)} %w_uq_hbm.1, bf16[1024,1024]{1,0:T(8,128)(2,1)} %w_out_hbm.1, ...), custom_call_target="tpu_custom_call" | custom-call | tf_op jit(solution)/shard_map/pallas_call | solution.py:385
  44.2 0.7 %copy.11 = bf16[1,64,1024]{2,1,0:T(8,128)(2,1)} copy(bf16[1,64,1024]{2,1,0:T(8,128)(2,1)S(1)} %bitcast.2) | data formatting | bytes 262144

commit v4 on v3

--- a/solution.py
+++ b/solution.py
@@ -30,7 +30,7 @@
 
 
 def ranked_hits(named, wanted):
-    shape = (2 * PAIR, PAIR)
+    shape = named.shape
     row = lax.broadcasted_iota(I32, shape, 0)
     lane = lax.broadcasted_iota(I32, shape, 1)
     half = lax.rem(lax.div(row, CAP), 2)
@@ -76,18 +76,20 @@
 
     z, x = lax.div(req, 4), lax.rem(req, 4)
     offsets = sorted(
-        [(dz, dx) for dz in range(4) for dx in range(4) if dz or dx],
-        key=lambda way: -min(way[0], 4 - way[0]) - min(way[1], 4 - way[1]),
+        [(dz, dx) for dz in range(4) for dx in range(4)],
+        key=lambda way: min(way[0], 4 - way[0]) + min(way[1], 4 - way[1]),
     )
     peers = [lax.rem(z + dz, 4) * 4 + lax.rem(x + dx, 4) for dz, dx in offsets]
-    for peer in peers:
-        pl.semaphore_signal(barrier, inc=1, device_id=(peer, ctx), device_id_type=MESH)
+    seen_from = [offsets.index((-dz % 4, -dx % 4)) for dz, dx in offsets]
+    others = range(OWNERS - 1, 0, -1)
+    for place in others:
+        pl.semaphore_signal(barrier, inc=1, device_id=(peers[place], ctx), device_id_type=MESH)
     for other in (partner, up * 2 + core, down * 2 + core, far * 2 + core):
         pl.semaphore_signal(barrier, inc=1, device_id=(req, other), device_id_type=MESH)
     asked_chip = jnp.where(core == 0, y, far)
     lanes = pl.ds(pl.multiple_of(asked_chip * PAIR, PAIR), PAIR)
     own_ids = [
-        pltpu.make_async_copy(src.at[:, lanes], ids.at[req, which], id_load.at[which])
+        pltpu.make_async_copy(src.at[:, lanes], ids.at[0, which], id_load.at[which])
         for which, src in enumerate((owner_hbm, slot_hbm))
     ]
     for copy in [*own_ids, *loads]:
@@ -96,18 +98,18 @@
         copy.wait()
     pl.semaphore_wait(barrier, OWNERS - 1 + 4)
 
-    def id_copy(peer, index):
-        return pltpu.make_async_remote_copy(
-            src_ref=ids.at[req],
-            dst_ref=ids.at[index],
-            send_sem=id_send.at[peer],
-            recv_sem=id_recv.at[index],
-            device_id=(peer, ctx),
-            device_id_type=MESH,
-        )
-
-    for peer in peers:
-        id_copy(peer, req).start()
+    def id_copy(place, there):
+        return pltpu.make_async_remote_copy(
+            src_ref=ids.at[0],
+            dst_ref=ids.at[there],
+            send_sem=id_send.at[place],
+            recv_sem=id_recv.at[there],
+            device_id=(peers[place], ctx),
+            device_id_type=MESH,
+        )
+
+    for place in others:
+        id_copy(place, seen_from[place]).start()
 
     def start_kv(head, carry):
         kv_copy(0, head).start()
@@ -117,39 +119,43 @@
     lax.fori_loop(0, HEADS, start_kv, 0)
     loads[0].wait()
 
-    def wait_ids(step, carry):
-        peer = lax.rem(req + step, OWNERS)
-        id_copy(peer, peer).wait_recv()
-        return carry
-
-    lax.fori_loop(1, OWNERS, wait_ids, 0)
-
-    wide = (OWNERS, 2 * CAP, PAIR)
-    named = jnp.broadcast_to(ids[:, 0], wide).reshape(2 * PAIR, PAIR)
-    asked = jnp.broadcast_to(ids[:, 1], wide).reshape(2 * PAIR, PAIR)
-    hits = ranked_hits(named, req)
-    chosen = jnp.sum(hits * asked.astype(F32), axis=1, keepdims=True).astype(I32)
-    onehot = jnp.where(
-        lax.broadcasted_iota(I32, (2 * PAIR, ITEMS), 1) == chosen, 1.0, 0.0
-    ).astype(BF16)
-    rows = jnp.dot(onehot, table[...], preferred_element_type=F32)
-    rowbuf[...] = rows.reshape(OWNERS, 2 * CAP, DE).astype(BF16)
-
-    def row_copy(peer, index):
-        return pltpu.make_async_remote_copy(
-            src_ref=rowbuf.at[peer],
-            dst_ref=got.at[index],
-            send_sem=row_send.at[peer],
-            recv_sem=row_recv.at[index],
-            device_id=(peer, ctx),
-            device_id_type=MESH,
-        )
-
-    for peer in peers:
-        row_copy(peer, req).start()
-    got[req] = rowbuf[req]
-
-    asked_here = jnp.broadcast_to(ids[req, 0], (2 * PAIR, PAIR))
+    def row_copy(place):
+        return pltpu.make_async_remote_copy(
+            src_ref=rowbuf.at[place],
+            dst_ref=got.at[req],
+            send_sem=row_send.at[place],
+            recv_sem=row_recv.at[req],
+            device_id=(peers[place], ctx),
+            device_id_type=MESH,
+        )
+
+    def look_up(first, count):
+        wide = (count, 2 * CAP, PAIR)
+        flat = (count * 2 * CAP, PAIR)
+        named = jnp.broadcast_to(ids[first : first + count, 0], wide).reshape(flat)
+        asked = jnp.broadcast_to(ids[first : first + count, 1], wide).reshape(flat)
+        hits = ranked_hits(named, req)
+        chosen = jnp.sum(hits * asked.astype(F32), axis=1, keepdims=True).astype(I32)
+        onehot = jnp.where(
+            lax.broadcasted_iota(I32, (flat[0], ITEMS), 1) == chosen, 1.0, 0.0
+        ).astype(BF16)
+        rows = jnp.dot(onehot, table[...], preferred_element_type=F32)
+        rowbuf[first : first + count] = rows.reshape(count, 2 * CAP, DE).astype(BF16)
+
+    near = 8
+    for place in range(1, near):
+        id_copy(place, place).wait_recv()
+    look_up(0, near)
+    for place in range(near - 1, 0, -1):
+        row_copy(place).start()
+    for place in range(near, OWNERS):
+        id_copy(place, place).wait_recv()
+    look_up(near, OWNERS - near)
+    for place in range(OWNERS - 1, near - 1, -1):
+        row_copy(place).start()
+    got[req] = rowbuf[0]
+
+    asked_here = jnp.broadcast_to(ids[0, 0], (2 * PAIR, PAIR))
     giver = lax.div(lax.broadcasted_iota(I32, (2 * PAIR, PAIR), 0), 2 * CAP)
     order = jnp.transpose(ranked_hits(asked_here, giver)).astype(BF16)
 
@@ -174,12 +180,18 @@
     for load in loads[1:]:
         load.wait()
 
-    def wait_rows(step, carry):
-        peer = lax.rem(req + step, OWNERS)
-        row_copy(peer, peer).wait_recv()
-        return carry
-
-    lax.fori_loop(1, OWNERS, wait_rows, 0)
+    def came(peer):
+        return pltpu.make_async_remote_copy(
+            src_ref=rowbuf.at[0],
+            dst_ref=got.at[peer],
+            send_sem=row_send.at[0],
+            recv_sem=row_recv.at[peer],
+            device_id=(peer, ctx),
+            device_id_type=MESH,
+        )
+
+    for place in others:
+        came(peers[place]).wait_recv()
     emb[core] = jnp.dot(
         order, got[...].reshape(2 * PAIR, DE), preferred_element_type=F32
     ).astype(BF16)
@@ -249,23 +261,23 @@
     piece = 512
     pieces = KEYS // piece
 
-    def attend_two(pair):
+    def attend_two(quad):
         def scored(item):
             start = (item % pieces) * piece
             return lax.dot_general(
-                keys[pair * 2 + item // pieces, start : start + piece, :],
-                query_wide[pair * 2 + item // pieces],
+                keys[quad * 4 + item // pieces, start : start + piece, :],
+                query_wide[quad * 4 + item // pieces],
                 (((1,), (1,)), ((), ())),
                 preferred_element_type=F32,
             )
 
         score = scored(0)
         total = None
-        for item in range(2 * pieces):
-            ahead = scored(item + 1) if item + 1 < 2 * pieces else None
+        for item in range(4 * pieces):
+            ahead = scored(item + 1) if item + 1 < 4 * pieces else None
             start = (item % pieces) * piece
             added = lax.dot_general(
-                vals[pair * 2 + item // pieces, start : start + piece, :],
+                vals[quad * 4 + item // pieces, start : start + piece, :],
                 weigh(score),
                 (((0,), (0,)), ((), ())),
                 preferred_element_type=F32,
@@ -274,13 +286,14 @@
             if item % pieces == pieces - 1:
                 turned = jnp.transpose(total)
                 acc[item // pieces] = turned[:PAIR]
-                acc[2 + item // pieces] = turned[PAIR:]
+                acc[4 + item // pieces] = turned[PAIR:]
             score = ahead
-        hand_over(2, pair, 0)
-        hand_over(3, pair, 2)
-
-    def attend_one(block, pair):
-        for head in range(2):
+        for side in range(2):
+            for part in range(2):
+                hand_over(2 + side, quad * 2 + part, 4 * side + 2 * part)
+
+    def attend_one(block, pair, count=1):
+        for head in range(2 * count):
             score = lax.dot_general(
                 query[block, pair * 2 + head],
                 keys[pair * 2 + head],
@@ -290,7 +303,8 @@
             acc[head] = jnp.dot(
                 weigh(score), vals[pair * 2 + head], preferred_element_type=F32
             )
-        hand_over(block, pair, 0)
+        for part in range(count):
+            hand_over(block, pair + part, 2 * part)
 
     def open_block(block):
         features, normed, scaled = project(emb[block])
@@ -306,40 +320,39 @@
         copy.start()
     open_block(1 - core)
 
-    def far_step(pair, carry):
-        attend_one(1, pair)
-        finish(1, pair - 1)
-        return carry
-
-    lax.fori_loop(1, 4, far_step, 0)
+    attend_one(1, 1, 3)
+    finish(1, 0)
 
     for copy in emb_copies:
         copy.wait_recv()
     keep_query(query_wide, project(emb[2:4].reshape(2 * PAIR, DE))[2])
 
-    def side_step(pair, carry):
-        attend_two(pair)
-
-        @pl.when(pair == 0)
+    def side_step(quad, carry):
+        attend_two(quad)
+
+        @pl.when(quad == 0)
         def _():
-            finish(1, 3)
-
-        @pl.when(pair > 0)
+            for pair in range(1, 4):
+                finish(1, pair)
+
+        @pl.when(quad == 1)
         def _():
-            finish(2, pair - 1)
-            finish(3, pair - 1)
+            for pair in range(2):
+                finish(2, pair)
+                finish(3, pair)
 
         return carry
 
-    lax.fori_loop(0, 4, side_step, 0)
+    lax.fori_loop(0, 2, side_step, 0)
 
     def own_step(pair, carry):
         attend_one(0, pair)
 
         @pl.when(pair == 1)
         def _():
-            finish(2, 3)
-            finish(3, 3)
+            for late in range(2, 4):
+                finish(2, late)
+                finish(3, late)
 
         return carry
 
@@ -362,13 +375,9 @@
     )
     out_ref[...] = ranked.astype(BF16)
 
-    def drain(step, carry):
-        peer = lax.rem(req + step, OWNERS)
-        id_copy(peer, req).wait_send()
-        row_copy(peer, req).wait_send()
-        return carry
-
-    lax.fori_loop(1, OWNERS, drain, 0)
+    for place in others:
+        id_copy(place, seen_from[place]).wait_send()
+        row_copy(place).wait_send()
     for copy in [emb_given, *emb_copies]:
         copy.wait_send()
     for pair in range(4):
@@ -402,7 +411,7 @@
             pltpu.VMEM((2, PAIR, WIDTH), BF16),
             pltpu.VMEM((2, HEADS, PAIR, DH), BF16),
             pltpu.VMEM((HEADS, 2 * PAIR, DH), BF16),
-            pltpu.VMEM((4, PAIR, DH), F32),
+            pltpu.VMEM((8, PAIR, DH), F32),
             pltpu.VMEM((4, HEADS, HALF, DH), F32),
             pltpu.VMEM((4, HEADS, HALF, DH), BF16),
             pltpu.VMEM((4, HEADS, HALF, DH), BF16),

time: 45.1 us -> 44.4 us (0.984)
  Pallas kernels: 43.6 us -> 43 us
    pallas_call x1, Pallas kernels: 43.6 us -> 43 us  [shards(): pl.pallas_call(kernel, out_shape=pltpu.VMEM((HALF, WIDTH), BF16), in_spec...]
where the time goes in v4:
time: 44.4 us; the launch traced here: 44.3 us
  Pallas kernels  43 us (97%)
  local copies, waits for them, and re-layouts  0.66 us (1%)
  between operations  0.66 us (1%)
    pallas_call x1, Pallas kernels, shards(): pl.pallas_call(kernel, out_shape=pltpu.VMEM((HALF, WIDTH), BF16), in_spec...  43 us

profile of v4, /device:TPU:1, one launch (start us, length us, event | category | flops | bytes accessed | tf_op | source)
XLA Modules:
  0.0 44.3 jit_solution(1425805757955385470)
XLA Ops:
  0.7 43.0 %shard_map.91 = bf16[64,1024]{1,0:T(8,128)(2,1)S(1)} custom-call(s32[1,512]{1,0:T(1,128)} %bitcast.3, s32[1,512]{1,0:T(1,128)} %slot_hbm.1, s32[1]{0:T(128)S(6)} %copy.12.len_ref, bf16[2048,256]{1,0:T(8,128)(2,1)} %table_hbm.1, bf16[256,1024]{1,0:T(8,128)(2,1)} %w_in_hbm.1, bf16[1024,2048]{1,0:T(8,128)(2,1)} %w_uq_hbm.1, bf16[1024,1024]{1,0:T(8,128)(2,1)} %w_out_hbm.1, ...), custom_call_target="tpu_custom_call" | custom-call | tf_op jit(solution)/shard_map/pallas_call | solution.py:394
  43.6 0.7 %copy.11 = bf16[1,64,1024]{2,1,0:T(8,128)(2,1)} copy(bf16[1,64,1024]{2,1,0:T(8,128)(2,1)S(1)} %bitcast.2) | data formatting | bytes 262144

commit v5 on v4

--- a/solution.py
+++ b/solution.py
@@ -142,7 +142,7 @@
         rows = jnp.dot(onehot, table[...], preferred_element_type=F32)
         rowbuf[first : first + count] = rows.reshape(count, 2 * CAP, DE).astype(BF16)
 
-    near = 8
+    near = 11
     for place in range(1, near):
         id_copy(place, place).wait_recv()
     look_up(0, near)
@@ -362,12 +362,15 @@
         jnp.dot(norm[0, my_rows, :], w_uq[:, :WIDTH], preferred_element_type=F32)
     ).astype(BF16)
     for pair in range(4):
-        swap_copy(0, pair).wait_recv()
         for block in range(1, 4):
             sum_copy(block, pair).wait_recv()
-    total = mine[0] + swapped[0].astype(F32)
-    for block in range(1, 4):
-        total = total + parts[block].astype(F32)
+    mine[0] = mine[0] + sum(parts[block].astype(F32) for block in range(1, 4))
+    for pair in range(3):
+        swap_copy(0, pair).wait_recv()
+    mine[0, :6] = mine[0, :6] + swapped[0, :6].astype(F32)
+    swap_copy(0, 3).wait_recv()
+    mine[0, 6:] = mine[0, 6:] + swapped[0, 6:].astype(F32)
+    total = mine[0]
     attended = jnp.concatenate([total[head] for head in range(HEADS)], axis=-1)
     mixed = (layer_norm(attended) * gate.astype(F32)).astype(BF16)
     ranked = feat[0, my_rows, :].astype(F32) + jnp.dot(

time: 44.4 us -> 44.4 us (level)
  no operation moved by 1% of the time
where the time goes in v5:
time: 44.4 us; the launch traced here: 44.3 us
  Pallas kernels  42.9 us (97%)
  local copies, waits for them, and re-layouts  0.66 us (1%)
  between operations  0.66 us (1%)
    pallas_call x1, Pallas kernels, shards(): pl.pallas_call(kernel, out_shape=pltpu.VMEM((HALF, WIDTH), BF16), in_spec...  42.9 us

profile of v5, /device:TPU:1, one launch (start us, length us, event | category | flops | bytes accessed | tf_op | source)
XLA Modules:
  0.0 44.3 jit_solution(15925277470138802581)
XLA Ops:
  0.7 42.9 %shard_map.91 = bf16[64,1024]{1,0:T(8,128)(2,1)S(1)} custom-call(s32[1,512]{1,0:T(1,128)} %bitcast.3, s32[1,512]{1,0:T(1,128)} %slot_hbm.1, s32[1]{0:T(128)S(6)} %copy.12.len_ref, bf16[2048,256]{1,0:T(8,128)(2,1)} %table_hbm.1, bf16[256,1024]{1,0:T(8,128)(2,1)} %w_in_hbm.1, bf16[1024,2048]{1,0:T(8,128)(2,1)} %w_uq_hbm.1, bf16[1024,1024]{1,0:T(8,128)(2,1)} %w_out_hbm.1, ...), custom_call_target="tpu_custom_call" | custom-call | tf_op jit(solution)/shard_map/pallas_call | solution.py:397
  43.6 0.7 %copy.11 = bf16[1,64,1024]{2,1,0:T(8,128)(2,1)} copy(bf16[1,64,1024]{2,1,0:T(8,128)(2,1)S(1)} %bitcast.2) | data formatting | bytes 262144
